TPU v7x, 128 devices: a whole 4x4x4 slice. The times are simulated.
128 devices in a mesh: section: 4 (over z), mp: 32 (over y, x, core).
Axes of the slice: x: 4, y: 4, z: 4, core: 2. Of those that a mesh axis runs over, the one named last changes fastest.
Arguments:
- entering_hidden: bfloat16 [4, 256, 8192], P('section', None, 'mp'), may hold values from -12 to 12
- section_weight: bfloat16 [4, 8192, 8192], P('section', None, 'mp'), may hold values from -0.0625 to 0.0625
- section_norm_gain: bfloat16 [4, 8192], P('section', 'mp'), may hold values from 0.5 to 1.5
- plugin_narrowing_factors: bfloat16 [4, 32, 8192, 64], P('section', 'mp'), may hold values from -0.0625 to 0.0625
- plugin_widening_factors: bfloat16 [4, 32, 64, 8192], P('section', 'mp'), may hold values from -0.75 to 0.75
- reward_head: bfloat16 [8192], P('mp'), may hold values from -0.0625 to 0.0625
- adapter_of_block: int32 [4, 2], replicated, may hold values from 0 to 31
- live_block_rows: int32 [4, 2], P('section'), may hold values from 1 to 128
Outputs:
- hidden_out: bfloat16 [4, 256, 8192], P('section', None, 'mp')
- scores: float32 [4, 256], P('section')
All inputs are finite; a program needn't handle non-finite values.
Results may differ from a plain program's by a relative error of at most 0.022.
Values may be sent and summed in bfloat16 or wider, within the bound.
A program may use at most 64 MiB of HBM per device.

v0:
```python
import jax
import jax.numpy as jnp
from jax import lax
from jax.sharding import PartitionSpec as P

BLOCK = 128


def shifted(value, axis, steps):
    count = lax.axis_size(axis)
    initial, last = (max(0, -steps), min(count, count - steps))
    return lax.ppermute(value, axis, [(source, source + steps) for source in range(initial, last)])


def shards(
    entering_hidden,
    section_weight,
    section_norm_gain,
    plugin_narrowing_factors,
    plugin_widening_factors,
    reward_head,
    adapter_of_block,
    live_block_rows,
):
    sections = lax.axis_size("section")
    section_index = lax.axis_index("section")
    owners = lax.axis_size("mp")
    owner_index = lax.axis_index("mp")
    batches_here, rows, piece_extent = entering_hidden.shape
    micro = batches_here * sections
    width = piece_extent * owners
    blocks = rows // BLOCK
    owned_blocks = plugin_narrowing_factors.shape[1]
    adapters = owned_blocks * owners
    rank_position = plugin_narrowing_factors.shape[3]
    weight = section_weight[0]
    gain = section_norm_gain[0].astype(jnp.float32)
    fed = lax.all_gather(entering_hidden, "section", axis=0, tiled=True)
    up_map_columns = lax.all_to_all(
        plugin_widening_factors, "mp", split_axis=3, concat_axis=1, tiled=True
    )[0]
    up_table = up_map_columns.reshape(adapters, rank_position * piece_extent)

    def layer_of_section(hidden_state, adapter_numbers):
        hidden_f = hidden_state.astype(jnp.float32)
        onehot = (
            adapter_numbers[:, None] == jnp.arange(adapters, dtype=jnp.int32)[None, :]
        ).astype(jnp.bfloat16)
        squares = lax.psum(jnp.sum(hidden_f * hidden_f, axis=1), "mp")
        rescaled_activation = (
            hidden_f * lax.rsqrt(squares / width + 1e-05)[:, None] * gain[None, :]
        ).astype(jnp.bfloat16)
        gathered = lax.all_gather(rescaled_activation, "mp", axis=1, tiled=True)
        base = jnp.dot(gathered, weight, preferred_element_type=jnp.float32)
        local_ids = adapter_numbers - owner_index * owned_blocks
        mine = (local_ids >= 0) & (local_ids < owned_blocks)
        products = []
        for block_number in range(blocks):
            segment = gathered[block_number * BLOCK : (block_number + 1) * BLOCK]
            picked = jnp.clip(local_ids[block_number], 0, owned_blocks - 1)
            products.append(
                lax.cond(
                    mine[block_number],
                    lambda incoming_rows, selected_adapter: jnp.dot(
                        incoming_rows,
                        plugin_narrowing_factors[0, selected_adapter],
                        preferred_element_type=jnp.float32,
                    ),
                    lambda incoming_rows, selected_adapter: jnp.zeros(
                        (BLOCK, rank_position), jnp.float32
                    ),
                    segment,
                    picked,
                )
            )
        compressed_projection = jnp.stack(products)
        compressed_projection = lax.psum(compressed_projection.astype(jnp.bfloat16), "mp")
        chosen_expansion_matrix = (
            jnp.dot(onehot, up_table, preferred_element_type=jnp.float32)
            .astype(jnp.bfloat16)
            .reshape(blocks, rank_position, piece_extent)
        )
        thin_correction = jnp.einsum(
            "sin,sny->siy",
            compressed_projection,
            chosen_expansion_matrix,
            preferred_element_type=jnp.float32,
        ).reshape(rows, piece_extent)
        return (hidden_f + base + 2.0 * thin_correction).astype(jnp.bfloat16)

    def tick(step, carry):
        moving, finished = carry
        arrived = shifted(moving, "section", 1)
        feed_now = lax.dynamic_index_in_dim(fed, jnp.minimum(step, micro - 1), 0, keepdims=False)
        current_signal = jnp.where(section_index == 0, feed_now, arrived)
        selected_adapter = step - section_index
        valid = (selected_adapter >= 0) & (selected_adapter < micro)
        position = jnp.clip(selected_adapter, 0, micro - 1)
        adapter_numbers = lax.dynamic_index_in_dim(adapter_of_block, position, 0, keepdims=False)
        output = layer_of_section(current_signal, adapter_numbers)
        entry_tuple = valid & (section_index == sections - 1)
        previous = lax.dynamic_index_in_dim(finished, position, 0, keepdims=False)
        finished = lax.dynamic_update_index_in_dim(
            finished, jnp.where(entry_tuple, output, previous), position, 0
        )
        return (output, finished)

    start_moving = jnp.zeros((rows, piece_extent), jnp.bfloat16)
    start_finished = jnp.zeros((micro, rows, piece_extent), jnp.bfloat16)
    moving, finished = lax.fori_loop(0, micro + sections - 1, tick, (start_moving, start_finished))
    hidden_out = lax.psum_scatter(
        finished.astype(jnp.float32).astype(jnp.bfloat16),
        "section",
        scatter_dimension=0,
        tiled=True,
    )
    partial_score = jnp.sum(
        hidden_out.astype(jnp.float32) * reward_head.astype(jnp.float32)[None, None, :], axis=2
    )
    raw = lax.psum(partial_score, "mp")
    place = jnp.arange(rows, dtype=jnp.int32) % BLOCK
    limits = jnp.repeat(live_block_rows, BLOCK, axis=1)
    scores = jnp.where(place[None, :] < limits, raw, jnp.float32(0.0))
    return (hidden_out, scores)


def solution(mesh):
    placed = (
        P("section", None, "mp"),
        P("section", None, "mp"),
        P("section", "mp"),
        P("section", "mp", None, None),
        P("section", "mp", None, None),
        P("mp"),
        P(),
        P("section", None),
    )
    return jax.shard_map(
        shards,
        mesh=mesh,
        in_specs=placed,
        out_specs=(P("section", None, "mp"), P("section", None)),
        check_vma=False,
    )
```

profile of v0, /device:TPU:0, one launch (start us, length us, event | category | flops | bytes accessed | tf_op | source)
XLA Modules:
  0.0 1954.4 jit_solution(13879705828689722286)
XLA Ops:
  17.7 45.2 %reduce.1 = bf16[8192,64]{1,0:T(8,128)(2,1)S(1)} reduce(bf16[8192,1,1,64]{3,2,1,0:T(2,128)(2,1)} %bitcast.80, bf16[]{:T(256)} %broadcast.105), dimensions={1,2}, to_apply=%bitcast.49.reduce_sub_computation | reduce | bytes 2097154
  106.2 1752.9 %while.17 = (s32[]{:T(128)}, bf16[256,256]{1,0:T(8,128)(2,1)}, bf16[4,256,256]{2,1,0:T(8,128)(2,1)}, pred[]{:T(512)}, bf16[4,256,256]{2,1,0:T(8,128)(2,1)}, /*in...) while((s32[]{:T(128)}, bf16[256,256]{1,0:T(8,128)(2,1)}, ...), condition=%wide.region_8.9_spmd.clone, body=%wide.region_0.8_spmd.clone.sunk | while | flops 1353712128 | bytes 31792572 | solution.py:110
  114.1 63.3 %psum.36 = f32[256]{0:T(256)S(1)} all-reduce(f32[256]{0:T(256)S(1)} %get-tuple-element.499), channel_id=1, replica_groups=mesh['section'=4,'mp'=32] {'mp'}, use_global_device_ids=true, to_apply=%region_2.2 | all-reduce | flops 256 | bytes 2048 | tf_op jit(solution)/shard_map/while/body/eval_jaxpr/psum | solution.py:49
  181.2 43.1 %all-gather.2.cloned.1.call-done = bf16[256,8192]{1,0:T(8,128)(2,1)} async-done(((bf16[256,256]{1,0:T(8,128)(2,1)}), bf16[256,8192]{1,0:T(8,128)(2,1)}) %all-gather.2.cloned.1.call-update) | async-done | bytes 4194320 | tf_op jit(solution)/shard_map/while/body/eval_jaxpr/all_gather | solution.py:53
  224.3 126.5 %psum.37 = bf16[2,128,64]{1,2,0:T(8,128)(2,1)S(1)} all-reduce(bf16[2,128,64]{1,2,0:T(8,128)(2,1)S(1)} %pad_maximum_fusion.2), channel_id=1, replica_groups=mesh['section'=4,'mp'=32] {'mp'}, use_global_device_ids=true, to_apply=%region_7.7 | all-reduce | flops 16384 | bytes 65536 | tf_op jit(solution)/shard_map/while/body/eval_jaxpr/psum | solution.py:77
  364.4 62.7 %psum.36 = f32[256]{0:T(256)S(1)} all-reduce(f32[256]{0:T(256)S(1)} %get-tuple-element.499), channel_id=1, replica_groups=mesh['section'=4,'mp'=32] {'mp'}, use_global_device_ids=true, to_apply=%region_2.2 | all-reduce | flops 256 | bytes 2048 | tf_op jit(solution)/shard_map/while/body/eval_jaxpr/psum | solution.py:49
  430.9 42.9 %all-gather.2.cloned.1.call-done = bf16[256,8192]{1,0:T(8,128)(2,1)} async-done(((bf16[256,256]{1,0:T(8,128)(2,1)}), bf16[256,8192]{1,0:T(8,128)(2,1)}) %all-gather.2.cloned.1.call-update) | async-done | bytes 4194320 | tf_op jit(solution)/shard_map/while/body/eval_jaxpr/all_gather | solution.py:53
  476.4 123.8 %psum.37 = bf16[2,128,64]{1,2,0:T(8,128)(2,1)S(1)} all-reduce(bf16[2,128,64]{1,2,0:T(8,128)(2,1)S(1)} %pad_maximum_fusion.2), channel_id=1, replica_groups=mesh['section'=4,'mp'=32] {'mp'}, use_global_device_ids=true, to_apply=%region_7.7 | all-reduce | flops 16384 | bytes 65536 | tf_op jit(solution)/shard_map/while/body/eval_jaxpr/psum | solution.py:77
  613.8 62.7 %psum.36 = f32[256]{0:T(256)S(1)} all-reduce(f32[256]{0:T(256)S(1)} %get-tuple-element.499), channel_id=1, replica_groups=mesh['section'=4,'mp'=32] {'mp'}, use_global_device_ids=true, to_apply=%region_2.2 | all-reduce | flops 256 | bytes 2048 | tf_op jit(solution)/shard_map/while/body/eval_jaxpr/psum | solution.py:49
  680.3 42.9 %all-gather.2.cloned.1.call-done = bf16[256,8192]{1,0:T(8,128)(2,1)} async-done(((bf16[256,256]{1,0:T(8,128)(2,1)}), bf16[256,8192]{1,0:T(8,128)(2,1)}) %all-gather.2.cloned.1.call-update) | async-done | bytes 4194320 | tf_op jit(solution)/shard_map/while/body/eval_jaxpr/all_gather | solution.py:53
  723.2 129.1 %psum.37 = bf16[2,128,64]{1,2,0:T(8,128)(2,1)S(1)} all-reduce(bf16[2,128,64]{1,2,0:T(8,128)(2,1)S(1)} %pad_maximum_fusion.2), channel_id=1, replica_groups=mesh['section'=4,'mp'=32] {'mp'}, use_global_device_ids=true, to_apply=%region_7.7 | all-reduce | flops 16384 | bytes 65536 | tf_op jit(solution)/shard_map/while/body/eval_jaxpr/psum | solution.py:77
  863.7 62.7 %psum.36 = f32[256]{0:T(256)S(1)} all-reduce(f32[256]{0:T(256)S(1)} %get-tuple-element.499), channel_id=1, replica_groups=mesh['section'=4,'mp'=32] {'mp'}, use_global_device_ids=true, to_apply=%region_2.2 | all-reduce | flops 256 | bytes 2048 | tf_op jit(solution)/shard_map/while/body/eval_jaxpr/psum | solution.py:49
  930.2 42.4 %all-gather.2.cloned.1.call-done = bf16[256,8192]{1,0:T(8,128)(2,1)} async-done(((bf16[256,256]{1,0:T(8,128)(2,1)}), bf16[256,8192]{1,0:T(8,128)(2,1)}) %all-gather.2.cloned.1.call-update) | async-done | bytes 4194320 | tf_op jit(solution)/shard_map/while/body/eval_jaxpr/all_gather | solution.py:53
  972.6 126.5 %psum.37 = bf16[2,128,64]{1,2,0:T(8,128)(2,1)S(1)} all-reduce(bf16[2,128,64]{1,2,0:T(8,128)(2,1)S(1)} %pad_maximum_fusion.2), channel_id=1, replica_groups=mesh['section'=4,'mp'=32] {'mp'}, use_global_device_ids=true, to_apply=%region_7.7 | all-reduce | flops 16384 | bytes 65536 | tf_op jit(solution)/shard_map/while/body/eval_jaxpr/psum | solution.py:77
  1115.3 62.7 %psum.36 = f32[256]{0:T(256)S(1)} all-reduce(f32[256]{0:T(256)S(1)} %get-tuple-element.499), channel_id=1, replica_groups=mesh['section'=4,'mp'=32] {'mp'}, use_global_device_ids=true, to_apply=%region_2.2 | all-reduce | flops 256 | bytes 2048 | tf_op jit(solution)/shard_map/while/body/eval_jaxpr/psum | solution.py:49
  1181.8 41.3 %all-gather.2.cloned.1.call-done = bf16[256,8192]{1,0:T(8,128)(2,1)} async-done(((bf16[256,256]{1,0:T(8,128)(2,1)}), bf16[256,8192]{1,0:T(8,128)(2,1)}) %all-gather.2.cloned.1.call-update) | async-done | bytes 4194320 | tf_op jit(solution)/shard_map/while/body/eval_jaxpr/all_gather | solution.py:53
  1223.1 126.5 %psum.37 = bf16[2,128,64]{1,2,0:T(8,128)(2,1)S(1)} all-reduce(bf16[2,128,64]{1,2,0:T(8,128)(2,1)S(1)} %pad_maximum_fusion.2), channel_id=1, replica_groups=mesh['section'=4,'mp'=32] {'mp'}, use_global_device_ids=true, to_apply=%region_7.7 | all-reduce | flops 16384 | bytes 65536 | tf_op jit(solution)/shard_map/while/body/eval_jaxpr/psum | solution.py:77
  1363.1 62.7 %psum.36 = f32[256]{0:T(256)S(1)} all-reduce(f32[256]{0:T(256)S(1)} %get-tuple-element.499), channel_id=1, replica_groups=mesh['section'=4,'mp'=32] {'mp'}, use_global_device_ids=true, to_apply=%region_2.2 | all-reduce | flops 256 | bytes 2048 | tf_op jit(solution)/shard_map/while/body/eval_jaxpr/psum | solution.py:49
  1429.6 45.5 %all-gather.2.cloned.1.call-done = bf16[256,8192]{1,0:T(8,128)(2,1)} async-done(((bf16[256,256]{1,0:T(8,128)(2,1)}), bf16[256,8192]{1,0:T(8,128)(2,1)}) %all-gather.2.cloned.1.call-update) | async-done | bytes 4194320 | tf_op jit(solution)/shard_map/while/body/eval_jaxpr/all_gather | solution.py:53
  1475.2 126.5 %psum.37 = bf16[2,128,64]{1,2,0:T(8,128)(2,1)S(1)} all-reduce(bf16[2,128,64]{1,2,0:T(8,128)(2,1)S(1)} %pad_maximum_fusion.2), channel_id=1, replica_groups=mesh['section'=4,'mp'=32] {'mp'}, use_global_device_ids=true, to_apply=%region_7.7 | all-reduce | flops 16384 | bytes 65536 | tf_op jit(solution)/shard_map/while/body/eval_jaxpr/psum | solution.py:77
  1615.2 62.7 %psum.36 = f32[256]{0:T(256)S(1)} all-reduce(f32[256]{0:T(256)S(1)} %get-tuple-element.499), channel_id=1, replica_groups=mesh['section'=4,'mp'=32] {'mp'}, use_global_device_ids=true, to_apply=%region_2.2 | all-reduce | flops 256 | bytes 2048 | tf_op jit(solution)/shard_map/while/body/eval_jaxpr/psum | solution.py:49
  1681.7 45.3 %all-gather.2.cloned.1.call-done = bf16[256,8192]{1,0:T(8,128)(2,1)} async-done(((bf16[256,256]{1,0:T(8,128)(2,1)}), bf16[256,8192]{1,0:T(8,128)(2,1)}) %all-gather.2.cloned.1.call-update) | async-done | bytes 4194320 | tf_op jit(solution)/shard_map/while/body/eval_jaxpr/all_gather | solution.py:53
  1727.0 126.5 %psum.37 = bf16[2,128,64]{1,2,0:T(8,128)(2,1)S(1)} all-reduce(bf16[2,128,64]{1,2,0:T(8,128)(2,1)S(1)} %pad_maximum_fusion.2), channel_id=1, replica_groups=mesh['section'=4,'mp'=32] {'mp'}, use_global_device_ids=true, to_apply=%region_7.7 | all-reduce | flops 16384 | bytes 65536 | tf_op jit(solution)/shard_map/while/body/eval_jaxpr/psum | solution.py:77
  1881.8 64.6 %psum.31 = f32[1,256]{1,0:T(1,128)S(1)} all-reduce(f32[1,256]{1,0:T(1,128)S(1)} %bitcast.87), channel_id=1, replica_groups=mesh['section'=4,'mp'=32] {'mp'}, use_global_device_ids=true, to_apply=%region_11.12 | all-reduce | flops 256 | bytes 2048 | tf_op jit(solution)/shard_map/psum | solution.py:120
  (165 shorter events, 195.2 us)
Async XLA Ops:
  62.9 11.8 copy-start.1
  62.9 11.9 copy-start.2
  62.9 11.9 copy-start
  65.2 24.6 %all-to-all-start = ((bf16[32,2,8192]{2,1,0:T(2,128)(2,1)}), bf16[32,2,8192]{2,1,0:T(2,128)(2,1)S(1)}, u32[]{:S(2)}, u32[]{:S(2)}) async-start(bf16[32,2,8192]{2,1,0:T(2,128)(2,1)} %reshape.80), calls=%async_computation | async-start | bytes 2097152 | tf_op jit(solution)/shard_map/all_to_all | solution.py:39
  106.2 1753.5 %copy-start.3 = (bf16[256]{0:T(256)(128)(2,1)S(1)}, bf16[256]{0:T(256)(128)(2,1)}, u32[]{:S(2)}) copy-start(bf16[256]{0:T(256)(128)(2,1)} %param.19) | copy-start | bytes 1540
  106.2 1840.2 %copy-start.4 = (s32[1,2]{1,0:T(1,128)S(1)}, s32[1,2]{1,0:T(1,128)}, u32[]{:S(2)}) copy-start(s32[1,2]{1,0:T(1,128)} %param.21) | copy-start | bytes 28
  106.2 118.1 %all-gather.2.cloned.1.call-start = ((), (), s32[]{:S(2)}) async-start(), calls=%async_computation.3 | async-start | bytes 4325376 | tf_op jit(solution)/shard_map/while/body/eval_jaxpr/all_gather | solution.py:53
  106.2 6.8 collective-permute-start
  356.4 117.3 %all-gather.2.cloned.1.call-start = ((), (), s32[]{:S(2)}) async-start(), calls=%async_computation.3 | async-start | bytes 4325376 | tf_op jit(solution)/shard_map/while/body/eval_jaxpr/all_gather | solution.py:53
  357.4 6.0 collective-permute-start
  605.9 117.3 %all-gather.2.cloned.1.call-start = ((), (), s32[]{:S(2)}) async-start(), calls=%async_computation.3 | async-start | bytes 4325376 | tf_op jit(solution)/shard_map/while/body/eval_jaxpr/all_gather | solution.py:53
  606.8 6.0 collective-permute-start
  857.9 114.7 %all-gather.2.cloned.1.call-start = ((), (), s32[]{:S(2)}) async-start(), calls=%async_computation.3 | async-start | bytes 4325376 | tf_op jit(solution)/shard_map/while/body/eval_jaxpr/all_gather | solution.py:53
  858.8 3.8 collective-permute-start
  1104.7 118.4 %all-gather.2.cloned.1.call-start = ((), (), s32[]{:S(2)}) async-start(), calls=%async_computation.3 | async-start | bytes 4325376 | tf_op jit(solution)/shard_map/while/body/eval_jaxpr/all_gather | solution.py:53
  1105.7 8.6 collective-permute-start
  1355.2 119.9 %all-gather.2.cloned.1.call-start = ((), (), s32[]{:S(2)}) async-start(), calls=%async_computation.3 | async-start | bytes 4325376 | tf_op jit(solution)/shard_map/while/body/eval_jaxpr/all_gather | solution.py:53
  1356.1 6.0 collective-permute-start
  1607.3 119.7 %all-gather.2.cloned.1.call-start = ((), (), s32[]{:S(2)}) async-start(), calls=%async_computation.3 | async-start | bytes 4325376 | tf_op jit(solution)/shard_map/while/body/eval_jaxpr/all_gather | solution.py:53
  1608.2 6.0 collective-permute-start
  1859.1 21.6 %reduce-scatter.2.cloned.1.call-start = ((), (), s32[]{:S(2)}) async-start(), calls=%async_computation.2 | async-start | bytes 655360 | tf_op jit(solution)/shard_map/reduce_scatter | solution.py:111
Sparse Core Ops, SparseCore 0:
  178.3 45.9 all-gather.1
  428.0 45.7 all-gather.1
  677.4 45.7 all-gather.1
  927.3 45.2 all-gather.1
  1178.9 44.1 all-gather.1
  1426.7 48.3 all-gather.1
  1678.8 48.1 all-gather.1
Sparse Core Ops, SparseCore 1:
  1862.5 18.2 reduce-scatter.1
where the time goes:
time: 1960 us; the launch traced here: 1950 us
  blocking collectives  1400 us (71%)
  waiting for transfers between devices  343 us (18%)
  other arithmetic  65.1 us (3%)
  matrix products  44.3 us (2%)
  local copies, waits for them, and re-layouts  41.1 us (2%)
  starting transfers between devices  32.5 us (2%)
    psum x7, blocking collectives, layer_of_section(): lax.psum(compressed_projection.astype(jnp.bfloat16), 'mp')  885 us
    psum x7, blocking collectives, layer_of_section(): squares = lax.psum(jnp.sum(hidden_f * hidden_f, axis=1), 'mp')  439 us
    all_gather x7, waiting for transfers between devices, layer_of_section(): gathered = lax.all_gather(rescaled_activation, 'mp', axis=1, tiled=True)  303 us
    psum x1, blocking collectives, shards(): raw = lax.psum(partial_score, 'mp')  64.6 us
    unnamed x2, other arithmetic  45.2 us
  transfers between devices with their start and end apart: 16, of which 16 were waited for; matrix products, arithmetic and copies ran while one was open for 1% of the time, Pallas kernels for 0%

commit v1 on v0

--- a/solution.py
+++ b/solution.py
@@ -74,7 +74,8 @@
                 )
             )
         compressed_projection = jnp.stack(products)
-        compressed_projection = lax.psum(compressed_projection.astype(jnp.bfloat16), "mp")
+        z_in = compressed_projection.astype(jnp.bfloat16)
+        compressed_projection = jnp.sum(jax.lax.all_gather(z_in, "mp"), axis=0)
         chosen_expansion_matrix = (
             jnp.dot(onehot, up_table, preferred_element_type=jnp.float32)
             .astype(jnp.bfloat16)

time: 1960 us -> 1400 us (0.71)
  blocking collectives: 1400 us -> 529 us
  waiting for transfers between devices: 343 us -> 643 us
    psum x7 -> x0, blocking collectives: 885 us -> none  [layer_of_section(): lax.psum(compressed_projection.astype(jnp.bfloat16), 'mp')]
    all_gather x0 -> x7, waiting for transfers between devices: none -> 290 us  [layer_of_section(): compressed_projection = jnp.sum(jax.lax.all_gather(z_in, 'mp'), axis=0)]
  transfers between devices with their start and end apart: 16 -> 23, of which waited for: 16 -> 23; matrix products, arithmetic and copies ran while one was open for 1% -> 1% of each run, Pallas kernels for 0% -> 0%
where the time goes in v1:
time: 1400 us; the launch traced here: 1390 us
  waiting for transfers between devices  643 us (46%)
  blocking collectives  529 us (38%)
  other arithmetic  73.7 us (5%)
  local copies, waits for them, and re-layouts  46.2 us (3%)
  matrix products  44.1 us (3%)
  starting transfers between devices  32.4 us (2%)
  between operations  15.3 us (1%)
    psum x7, blocking collectives, layer_of_section(): squares = lax.psum(jnp.sum(hidden_f * hidden_f, axis=1), 'mp')  449 us
    all_gather x7, waiting for transfers between devices, layer_of_section(): gathered = lax.all_gather(rescaled_activation, 'mp', axis=1, tiled=True)  307 us
    all_gather x7, waiting for transfers between devices, layer_of_section(): compressed_projection = jnp.sum(jax.lax.all_gather(z_in, 'mp'), axis=0)  290 us
    psum x1, blocking collectives, shards(): raw = lax.psum(partial_score, 'mp')  64.6 us
    unnamed x2, other arithmetic  45.2 us
    dot_general x7, matrix products, layer_of_section(): base = jnp.dot(gathered, weight, preferred_element_type=jnp.float32)  37.7 us
  transfers between devices with their start and end apart: 23, of which 23 were waited for; matrix products, arithmetic and copies ran while one was open for 1% of the time, Pallas kernels for 0%

profile of v1, /device:TPU:0, one launch (start us, length us, event | category | flops | bytes accessed | tf_op | source)
XLA Modules:
  0.0 1394.1 jit_solution(7109522286773128321)
XLA Ops:
  17.7 45.2 %reduce.7 = bf16[8192,64]{1,0:T(8,128)(2,1)S(1)} reduce(bf16[8192,1,1,64]{3,2,1,0:T(2,128)(2,1)} %bitcast.80, bf16[]{:T(256)} %broadcast.115), dimensions={1,2}, to_apply=%bitcast.49.reduce_sub_computation | reduce | bytes 2097154
  106.2 1189.9 %while.18 = (s32[]{:T(128)}, bf16[256,256]{1,0:T(8,128)(2,1)S(1)}, bf16[4,256,256]{2,1,0:T(8,128)(2,1)}, pred[]{:T(512)}, bf16[4,256,256]{2,1,0:T(8,128)(2,1)}, ...) while((s32[]{:T(128)}, bf16[256,256]{1,0:T(8,128)(2,1)S(1)}, ...), condition=%wide.region_8.9_spmd.clone, body=%wide.region_0.8_spmd.clone.sunk | while | flops 1354203648 | bytes 36052464 | solution.py:111
  114.1 63.3 %psum.24 = f32[256]{0:T(256)S(1)} all-reduce(f32[256]{0:T(256)S(1)} %get-tuple-element.542), channel_id=1, replica_groups=mesh['section'=4,'mp'=32] {'mp'}, use_global_device_ids=true, to_apply=%region_2.2 | all-reduce | flops 256 | bytes 2048 | tf_op jit(solution)/shard_map/while/body/eval_jaxpr/psum | solution.py:49
  180.3 44.0 %all-gather.3.cloned.1.call-done = bf16[256,8192]{1,0:T(8,128)(2,1)} async-done(((bf16[256,256]{1,0:T(8,128)(2,1)}), bf16[256,8192]{1,0:T(8,128)(2,1)}) %all-gather.3.cloned.1.call-update) | async-done | bytes 4194320 | tf_op jit(solution)/shard_map/while/body/eval_jaxpr/all_gather | solution.py:53
  226.9 41.9 %all-gather.5.cloned.1.call-done = bf16[32,2,128,64]{2,3,1,0:T(8,128)(2,1)} async-done(((bf16[1,2,128,64]{2,3,1,0:T(8,128)(2,1)}), bf16[32,2,128,64]{2,3,1,0:T(8,128)(2,1)}) %all-gather.5.cloned.1.call-update) | async-done | bytes 1048592 | tf_op jit(solution)/shard_map/while/body/eval_jaxpr/all_gather | solution.py:78
  283.4 64.3 %psum.24 = f32[256]{0:T(256)S(1)} all-reduce(f32[256]{0:T(256)S(1)} %get-tuple-element.542), channel_id=1, replica_groups=mesh['section'=4,'mp'=32] {'mp'}, use_global_device_ids=true, to_apply=%region_2.2 | all-reduce | flops 256 | bytes 2048 | tf_op jit(solution)/shard_map/while/body/eval_jaxpr/psum | solution.py:49
  350.7 43.8 %all-gather.3.cloned.1.call-done = bf16[256,8192]{1,0:T(8,128)(2,1)} async-done(((bf16[256,256]{1,0:T(8,128)(2,1)}), bf16[256,8192]{1,0:T(8,128)(2,1)}) %all-gather.3.cloned.1.call-update) | async-done | bytes 4194320 | tf_op jit(solution)/shard_map/while/body/eval_jaxpr/all_gather | solution.py:53
  399.7 39.3 %all-gather.5.cloned.1.call-done = bf16[32,2,128,64]{2,3,1,0:T(8,128)(2,1)} async-done(((bf16[1,2,128,64]{2,3,1,0:T(8,128)(2,1)}), bf16[32,2,128,64]{2,3,1,0:T(8,128)(2,1)}) %all-gather.5.cloned.1.call-update) | async-done | bytes 1048592 | tf_op jit(solution)/shard_map/while/body/eval_jaxpr/all_gather | solution.py:78
  453.6 64.3 %psum.24 = f32[256]{0:T(256)S(1)} all-reduce(f32[256]{0:T(256)S(1)} %get-tuple-element.542), channel_id=1, replica_groups=mesh['section'=4,'mp'=32] {'mp'}, use_global_device_ids=true, to_apply=%region_2.2 | all-reduce | flops 256 | bytes 2048 | tf_op jit(solution)/shard_map/while/body/eval_jaxpr/psum | solution.py:49
  520.8 43.8 %all-gather.3.cloned.1.call-done = bf16[256,8192]{1,0:T(8,128)(2,1)} async-done(((bf16[256,256]{1,0:T(8,128)(2,1)}), bf16[256,8192]{1,0:T(8,128)(2,1)}) %all-gather.3.cloned.1.call-update) | async-done | bytes 4194320 | tf_op jit(solution)/shard_map/while/body/eval_jaxpr/all_gather | solution.py:53
  567.2 41.9 %all-gather.5.cloned.1.call-done = bf16[32,2,128,64]{2,3,1,0:T(8,128)(2,1)} async-done(((bf16[1,2,128,64]{2,3,1,0:T(8,128)(2,1)}), bf16[32,2,128,64]{2,3,1,0:T(8,128)(2,1)}) %all-gather.5.cloned.1.call-update) | async-done | bytes 1048592 | tf_op jit(solution)/shard_map/while/body/eval_jaxpr/all_gather | solution.py:78
  623.8 64.3 %psum.24 = f32[256]{0:T(256)S(1)} all-reduce(f32[256]{0:T(256)S(1)} %get-tuple-element.542), channel_id=1, replica_groups=mesh['section'=4,'mp'=32] {'mp'}, use_global_device_ids=true, to_apply=%region_2.2 | all-reduce | flops 256 | bytes 2048 | tf_op jit(solution)/shard_map/while/body/eval_jaxpr/psum | solution.py:49
  691.0 43.8 %all-gather.3.cloned.1.call-done = bf16[256,8192]{1,0:T(8,128)(2,1)} async-done(((bf16[256,256]{1,0:T(8,128)(2,1)}), bf16[256,8192]{1,0:T(8,128)(2,1)}) %all-gather.3.cloned.1.call-update) | async-done | bytes 4194320 | tf_op jit(solution)/shard_map/while/body/eval_jaxpr/all_gather | solution.py:53
  737.4 41.9 %all-gather.5.cloned.1.call-done = bf16[32,2,128,64]{2,3,1,0:T(8,128)(2,1)} async-done(((bf16[1,2,128,64]{2,3,1,0:T(8,128)(2,1)}), bf16[32,2,128,64]{2,3,1,0:T(8,128)(2,1)}) %all-gather.5.cloned.1.call-update) | async-done | bytes 1048592 | tf_op jit(solution)/shard_map/while/body/eval_jaxpr/all_gather | solution.py:78
  794.0 64.3 %psum.24 = f32[256]{0:T(256)S(1)} all-reduce(f32[256]{0:T(256)S(1)} %get-tuple-element.542), channel_id=1, replica_groups=mesh['section'=4,'mp'=32] {'mp'}, use_global_device_ids=true, to_apply=%region_2.2 | all-reduce | flops 256 | bytes 2048 | tf_op jit(solution)/shard_map/while/body/eval_jaxpr/psum | solution.py:49
  861.2 43.8 %all-gather.3.cloned.1.call-done = bf16[256,8192]{1,0:T(8,128)(2,1)} async-done(((bf16[256,256]{1,0:T(8,128)(2,1)}), bf16[256,8192]{1,0:T(8,128)(2,1)}) %all-gather.3.cloned.1.call-update) | async-done | bytes 4194320 | tf_op jit(solution)/shard_map/while/body/eval_jaxpr/all_gather | solution.py:53
  907.5 41.8 %all-gather.5.cloned.1.call-done = bf16[32,2,128,64]{2,3,1,0:T(8,128)(2,1)} async-done(((bf16[1,2,128,64]{2,3,1,0:T(8,128)(2,1)}), bf16[32,2,128,64]{2,3,1,0:T(8,128)(2,1)}) %all-gather.5.cloned.1.call-update) | async-done | bytes 1048592 | tf_op jit(solution)/shard_map/while/body/eval_jaxpr/all_gather | solution.py:78
  964.0 64.3 %psum.24 = f32[256]{0:T(256)S(1)} all-reduce(f32[256]{0:T(256)S(1)} %get-tuple-element.542), channel_id=1, replica_groups=mesh['section'=4,'mp'=32] {'mp'}, use_global_device_ids=true, to_apply=%region_2.2 | all-reduce | flops 256 | bytes 2048 | tf_op jit(solution)/shard_map/while/body/eval_jaxpr/psum | solution.py:49
  1031.2 43.8 %all-gather.3.cloned.1.call-done = bf16[256,8192]{1,0:T(8,128)(2,1)} async-done(((bf16[256,256]{1,0:T(8,128)(2,1)}), bf16[256,8192]{1,0:T(8,128)(2,1)}) %all-gather.3.cloned.1.call-update) | async-done | bytes 4194320 | tf_op jit(solution)/shard_map/while/body/eval_jaxpr/all_gather | solution.py:53
  1077.6 41.6 %all-gather.5.cloned.1.call-done = bf16[32,2,128,64]{2,3,1,0:T(8,128)(2,1)} async-done(((bf16[1,2,128,64]{2,3,1,0:T(8,128)(2,1)}), bf16[32,2,128,64]{2,3,1,0:T(8,128)(2,1)}) %all-gather.5.cloned.1.call-update) | async-done | bytes 1048592 | tf_op jit(solution)/shard_map/while/body/eval_jaxpr/all_gather | solution.py:78
  1133.9 64.3 %psum.24 = f32[256]{0:T(256)S(1)} all-reduce(f32[256]{0:T(256)S(1)} %get-tuple-element.542), channel_id=1, replica_groups=mesh['section'=4,'mp'=32] {'mp'}, use_global_device_ids=true, to_apply=%region_2.2 | all-reduce | flops 256 | bytes 2048 | tf_op jit(solution)/shard_map/while/body/eval_jaxpr/psum | solution.py:49
  1201.1 43.8 %all-gather.3.cloned.1.call-done = bf16[256,8192]{1,0:T(8,128)(2,1)} async-done(((bf16[256,256]{1,0:T(8,128)(2,1)}), bf16[256,8192]{1,0:T(8,128)(2,1)}) %all-gather.3.cloned.1.call-update) | async-done | bytes 4194320 | tf_op jit(solution)/shard_map/while/body/eval_jaxpr/all_gather | solution.py:53
  1247.5 41.5 %all-gather.5.cloned.1.call-done = bf16[32,2,128,64]{2,3,1,0:T(8,128)(2,1)} async-done(((bf16[1,2,128,64]{2,3,1,0:T(8,128)(2,1)}), bf16[32,2,128,64]{2,3,1,0:T(8,128)(2,1)}) %all-gather.5.cloned.1.call-update) | async-done | bytes 1048592 | tf_op jit(solution)/shard_map/while/body/eval_jaxpr/all_gather | solution.py:78
  1321.7 64.6 %psum.21 = f32[1,256]{1,0:T(1,128)S(1)} all-reduce(f32[1,256]{1,0:T(1,128)S(1)} %bitcast.87), channel_id=1, replica_groups=mesh['section'=4,'mp'=32] {'mp'}, use_global_device_ids=true, to_apply=%region_11.12 | all-reduce | flops 256 | bytes 2048 | tf_op jit(solution)/shard_map/psum | solution.py:121
  (186 shorter events, 215.4 us)
Async XLA Ops:
  65.2 24.6 %all-to-all-start = ((bf16[32,2,8192]{2,1,0:T(2,128)(2,1)}), bf16[32,2,8192]{2,1,0:T(2,128)(2,1)S(1)}, u32[]{:S(2)}, u32[]{:S(2)}) async-start(bf16[32,2,8192]{2,1,0:T(2,128)(2,1)} %reshape.119), calls=%async_computation | async-start | bytes 2097152 | tf_op jit(solution)/shard_map/all_to_all | solution.py:39
  106.2 1280.1 %copy-start.4 = (s32[1,2]{1,0:T(1,128)S(1)}, s32[1,2]{1,0:T(1,128)}, u32[]{:S(2)}) copy-start(s32[1,2]{1,0:T(1,128)} %param.21) | copy-start | bytes 28
  106.2 118.1 %all-gather.3.cloned.1.call-start = ((), (), s32[]{:S(2)}) async-start(), calls=%async_computation.3 | async-start | bytes 4325376 | tf_op jit(solution)/shard_map/while/body/eval_jaxpr/all_gather | solution.py:53
  106.2 6.8 collective-permute-start
  178.2 90.6 %all-gather.5.cloned.1.call-start = ((), (), s32[]{:S(2)}) async-start(), calls=%async_computation.4 | async-start | bytes 1081344 | tf_op jit(solution)/shard_map/while/body/eval_jaxpr/all_gather | solution.py:78
  275.8 118.7 %all-gather.3.cloned.1.call-start = ((), (), s32[]{:S(2)}) async-start(), calls=%async_computation.3 | async-start | bytes 4325376 | tf_op jit(solution)/shard_map/while/body/eval_jaxpr/all_gather | solution.py:53
  275.8 6.6 collective-permute-start
  348.5 90.4 %all-gather.5.cloned.1.call-start = ((), (), s32[]{:S(2)}) async-start(), calls=%async_computation.4 | async-start | bytes 1081344 | tf_op jit(solution)/shard_map/while/body/eval_jaxpr/all_gather | solution.py:78
  446.0 118.7 %all-gather.3.cloned.1.call-start = ((), (), s32[]{:S(2)}) async-start(), calls=%async_computation.3 | async-start | bytes 4325376 | tf_op jit(solution)/shard_map/while/body/eval_jaxpr/all_gather | solution.py:53
  446.0 6.6 collective-permute-start
  518.7 90.4 %all-gather.5.cloned.1.call-start = ((), (), s32[]{:S(2)}) async-start(), calls=%async_computation.4 | async-start | bytes 1081344 | tf_op jit(solution)/shard_map/while/body/eval_jaxpr/all_gather | solution.py:78
  616.2 118.7 %all-gather.3.cloned.1.call-start = ((), (), s32[]{:S(2)}) async-start(), calls=%async_computation.3 | async-start | bytes 4325376 | tf_op jit(solution)/shard_map/while/body/eval_jaxpr/all_gather | solution.py:53
  616.2 6.6 collective-permute-start
  688.9 90.4 %all-gather.5.cloned.1.call-start = ((), (), s32[]{:S(2)}) async-start(), calls=%async_computation.4 | async-start | bytes 1081344 | tf_op jit(solution)/shard_map/while/body/eval_jaxpr/all_gather | solution.py:78
  786.3 118.7 %all-gather.3.cloned.1.call-start = ((), (), s32[]{:S(2)}) async-start(), calls=%async_computation.3 | async-start | bytes 4325376 | tf_op jit(solution)/shard_map/while/body/eval_jaxpr/all_gather | solution.py:53
  786.3 6.6 collective-permute-start
  859.1 90.3 %all-gather.5.cloned.1.call-start = ((), (), s32[]{:S(2)}) async-start(), calls=%async_computation.4 | async-start | bytes 1081344 | tf_op jit(solution)/shard_map/while/body/eval_jaxpr/all_gather | solution.py:78
  956.4 118.7 %all-gather.3.cloned.1.call-start = ((), (), s32[]{:S(2)}) async-start(), calls=%async_computation.3 | async-start | bytes 4325376 | tf_op jit(solution)/shard_map/while/body/eval_jaxpr/all_gather | solution.py:53
  956.4 6.6 collective-permute-start
  1029.1 90.1 %all-gather.5.cloned.1.call-start = ((), (), s32[]{:S(2)}) async-start(), calls=%async_computation.4 | async-start | bytes 1081344 | tf_op jit(solution)/shard_map/while/body/eval_jaxpr/all_gather | solution.py:78
  1126.2 118.7 %all-gather.3.cloned.1.call-start = ((), (), s32[]{:S(2)}) async-start(), calls=%async_computation.3 | async-start | bytes 4325376 | tf_op jit(solution)/shard_map/while/body/eval_jaxpr/all_gather | solution.py:53
  1126.3 6.6 collective-permute-start
  1199.0 90.1 %all-gather.5.cloned.1.call-start = ((), (), s32[]{:S(2)}) async-start(), calls=%async_computation.4 | async-start | bytes 1081344 | tf_op jit(solution)/shard_map/while/body/eval_jaxpr/all_gather | solution.py:78
  1296.1 24.6 %reduce-scatter.2.cloned.1.call-start = ((), (), s32[]{:S(2)}) async-start(), calls=%async_computation.2 | async-start | bytes 655360 | tf_op jit(solution)/shard_map/reduce_scatter | solution.py:112
  (4 other events, 1226.0 us)
Sparse Core Ops, SparseCore 0:
  178.3 45.9 all-gather.2
  226.5 42.1 all-gather.4
  348.7 45.7 all-gather.2
  397.9 41.0 all-gather.4
  518.8 45.7 all-gather.2
  566.8 42.3 all-gather.4
  689.0 45.7 all-gather.2
  737.1 42.1 all-gather.4
  859.2 45.7 all-gather.2
  907.1 42.2 all-gather.4
  1029.2 45.7 all-gather.2
  1077.2 42.0 all-gather.4
  1199.1 45.7 all-gather.2
  1247.0 41.9 all-gather.4
Sparse Core Ops, SparseCore 1:
  1299.5 21.2 reduce-scatter.1
